TPU v7x, 32 devices: a whole 2x2x4 slice. The times are simulated.
32 devices in a mesh: fsdp: 8 (over z, y), rep: 4 (over x, core).
Axes of the slice: x: 2, y: 2, z: 4, core: 2. Of those that a mesh axis runs over, the one named last changes fastest.
Arguments:
- tokens: bfloat16 [64, 512, 768], P(('fsdp', 'rep')), may hold values from -6 to 6
- page_ids: int32 [64, 512], P(('fsdp', 'rep')), may hold values from 0 to 7, never falling along the last dimension, each value on 1 to 128 neighbouring positions
- box_coords: int32 [8, 64, 512], P(None, ('fsdp', 'rep')), may hold values from 0 to 1000
- w_qkv: bfloat16 [768, 2304], P('fsdp'), may hold values from -0.3125 to 0.3125
- b_qkv: bfloat16 [2304], P('fsdp'), may hold values from -3 to 3
- w_pos: bfloat16 [24576], P('fsdp'), may hold values from -0.75 to 0.75
- w_out: bfloat16 [768, 768], P('fsdp'), may hold values from -0.875 to 0.875
- b_out: bfloat16 [768], P('fsdp'), may hold values from -3 to 3
- gain_one: bfloat16 [768], P('fsdp'), may hold values from 0.5 to 1.5
- shift_one: bfloat16 [768], P('fsdp'), may hold values from -3 to 3
- w_up: bfloat16 [768, 3072], P('fsdp'), may hold values from -0.21875 to 0.21875
- b_up: bfloat16 [3072], P('fsdp'), may hold values from -3 to 3
- w_down: bfloat16 [3072, 768], P('fsdp'), may hold values from -0.109375 to 0.109375
- b_down: bfloat16 [768], P('fsdp'), may hold values from -3 to 3
- gain_two: bfloat16 [768], P('fsdp'), may hold values from 0.5 to 1.5
- shift_two: bfloat16 [768], P('fsdp'), may hold values from -3 to 3
- cotangent: bfloat16 [64, 512, 768], P(('fsdp', 'rep')), may hold values from -6 to 6
Outputs:
- layer_out: bfloat16 [64, 512, 768], P(('fsdp', 'rep'))
- grad_tokens: bfloat16 [64, 512, 768], P(('fsdp', 'rep'))
- grad_w_qkv: float32 [768, 2304], P('fsdp')
- grad_b_qkv: float32 [2304], P('fsdp')
- grad_w_pos: float32 [24576], P('fsdp')
- grad_w_out: float32 [768, 768], P('fsdp')
- grad_b_out: float32 [768], P('fsdp')
- grad_gain_one: float32 [768], P('fsdp')
- grad_shift_one: float32 [768], P('fsdp')
- grad_w_up: float32 [768, 3072], P('fsdp')
- grad_b_up: float32 [3072], P('fsdp')
- grad_w_down: float32 [3072, 768], P('fsdp')
- grad_b_down: float32 [768], P('fsdp')
- grad_gain_two: float32 [768], P('fsdp')
- grad_shift_two: float32 [768], P('fsdp')
Inputs may be any that keep to these rules, and one draw needn't show every extreme that they name: `page_ids`: within a row page ids never fall; every page holds 1 to 128 tokens, and one page of every row exactly 128.
All inputs are finite; a program needn't handle non-finite values.
Results may differ from a plain program's by a relative error of at most 0.017.
Values may be sent and summed in bfloat16 or wider, within the bound.
No kernel may reach another device: no remote copies, remote signals or barrier semaphores. Data moves between devices by JAX's collectives and lax.ppermute only.
A program may use at most 256 MiB of HBM per device.

v0:
```python
import math
import jax
import jax.numpy as jnp
from jax import lax
from jax.sharding import PartitionSpec as P

HEADS = 12
HD = 64
PE = 192
norm_eps = 1e-12


def layer_norm(values, gain, shift):
    center = jnp.mean(values, axis=-1, keepdims=True)
    offset = values - center
    spread = jnp.mean(offset * offset, axis=-1, keepdims=True)
    return offset * lax.rsqrt(spread + norm_eps) * gain + shift


def gelu_exact(values):
    return jax.nn.gelu(values, approximate=False)


def pair_swap(matrix):
    return matrix.reshape(PE // 2, 2, matrix.shape[-1])[:, ::-1].reshape(PE, matrix.shape[-1])


def row_scores(left_side, right_side, row_pages, score_scale):
    logits = jnp.einsum("hie,hje->hij", left_side, right_side, preferred_element_type=jnp.float32)
    same_page = row_pages[:, None] == row_pages[None, :]
    return jnp.where(same_page[None], logits * score_scale, -1e30)


def attend_row(left_side, right_side, value_heads, row_pages, score_scale):
    scores = row_scores(left_side, right_side, row_pages, score_scale)
    row_max = jnp.max(scores, axis=-1, keepdims=True)
    row_total = jnp.sum(jnp.exp(scores - row_max), axis=-1, keepdims=True)
    log_total = row_max + jnp.log(row_total)
    probs_low = jnp.exp(scores - log_total).astype(jnp.bfloat16)
    context = jnp.einsum("hij,hjd->hid", probs_low, value_heads, preferred_element_type=jnp.float32)
    return (context, log_total)


def attend_back(left_side, right_side, value_heads, row_pages, log_total, grad_ctx, score_scale):
    scores = row_scores(left_side, right_side, row_pages, score_scale)
    attn_probs = jnp.exp(scores - log_total)
    probs_low = attn_probs.astype(jnp.bfloat16)
    grad_probs = jnp.einsum(
        "hid,hjd->hij", grad_ctx, value_heads, preferred_element_type=jnp.float32
    )
    inner_sum = jnp.sum(grad_probs * attn_probs, axis=-1, keepdims=True)
    grad_logits = (attn_probs * (grad_probs - inner_sum) * score_scale).astype(jnp.bfloat16)
    grad_left = jnp.einsum(
        "hij,hje->hie", grad_logits, right_side, preferred_element_type=jnp.float32
    )
    grad_right = jnp.einsum(
        "hij,hie->hje", grad_logits, left_side, preferred_element_type=jnp.float32
    )
    grad_values = jnp.einsum(
        "hij,hid->hjd", probs_low, grad_ctx, preferred_element_type=jnp.float32
    )
    return (grad_left, grad_right, grad_values)


def body(
    tokens,
    page_ids,
    box_coords,
    w_qkv,
    b_qkv,
    w_pos,
    w_out,
    b_out,
    gain_one,
    shift_one,
    w_up,
    b_up,
    w_down,
    b_down,
    gain_two,
    shift_two,
    cotangent,
):
    row_count, seq_len, model_width = tokens.shape
    tok_count = row_count * seq_len
    score_scale = 1.0 / math.sqrt(HD + 2 * PE)
    shards = (
        w_qkv,
        w_out,
        w_up,
        w_down,
        b_qkv,
        w_pos,
        b_out,
        gain_one,
        shift_one,
        b_up,
        b_down,
        gain_two,
        shift_two,
    )
    gathered = (
        lax.all_gather(shards[0], "fsdp", axis=0, tiled=True),
        lax.all_gather(shards[1], "fsdp", axis=0, tiled=True),
        lax.all_gather(shards[2], "fsdp", axis=0, tiled=True),
        lax.all_gather(shards[3], "fsdp", axis=0, tiled=True),
        lax.all_gather(shards[4], "fsdp", axis=0, tiled=True),
        lax.all_gather(shards[5], "fsdp", axis=0, tiled=True),
        lax.all_gather(shards[6], "fsdp", axis=0, tiled=True),
        lax.all_gather(shards[7], "fsdp", axis=0, tiled=True),
        lax.all_gather(shards[8], "fsdp", axis=0, tiled=True),
        lax.all_gather(shards[9], "fsdp", axis=0, tiled=True),
        lax.all_gather(shards[10], "fsdp", axis=0, tiled=True),
        lax.all_gather(shards[11], "fsdp", axis=0, tiled=True),
        lax.all_gather(shards[12], "fsdp", axis=0, tiled=True),
    )
    (
        full_qkv,
        full_out,
        full_up,
        full_down,
        bias_qkv,
        pos_flat,
        bias_out,
        gain_first,
        shift_first,
        bias_up,
        bias_down,
        gain_second,
        shift_second,
    ) = gathered
    pos_all = pos_flat.reshape(2, PE, HD)

    def to_heads(flat_in):
        return flat_in.reshape(row_count, seq_len, HEADS, HD).transpose(0, 2, 1, 3)

    def from_heads(head_in):
        return head_in.transpose(0, 2, 1, 3).reshape(tok_count, model_width)

    flat_rows = tokens.reshape(tok_count, model_width)
    qkv_low = (
        jnp.dot(flat_rows, full_qkv, preferred_element_type=jnp.float32)
        + bias_qkv.astype(jnp.float32)
    ).astype(jnp.bfloat16)
    query_heads = to_heads(qkv_low[:, :model_width])
    key_heads = to_heads(qkv_low[:, model_width : 2 * model_width])
    value_heads = to_heads(qkv_low[:, 2 * model_width :])
    freq_count = PE // 16
    freq_vals = jnp.exp(
        jnp.arange(freq_count).astype(jnp.float32) * (-math.log(10000.0) / freq_count)
    )
    angles = jnp.moveaxis(box_coords, 0, -1).astype(jnp.float32)[..., None] * freq_vals
    sin_vals = jnp.sin(angles)
    cos_vals = jnp.cos(angles)
    feat_shape = (row_count, 1, seq_len, PE)
    box_feats = jnp.stack([sin_vals, cos_vals], axis=-1).reshape(feat_shape)
    sin_rep = jnp.stack([sin_vals, sin_vals], axis=-1).reshape(feat_shape)
    cos_sign = jnp.stack([-cos_vals, cos_vals], axis=-1).reshape(feat_shape)
    comb_query = jnp.concatenate([pos_all[1], pair_swap(pos_all[1])], axis=0)
    comb_key = jnp.concatenate([pos_all[0], pair_swap(pos_all[0])], axis=0)
    query_pos = jnp.einsum(
        "rhld,fd->rhlf", query_heads, comb_query, preferred_element_type=jnp.float32
    )
    key_pos = jnp.einsum("rhld,fd->rhlf", key_heads, comb_key, preferred_element_type=jnp.float32)
    turned_query = query_pos[..., PE:] * sin_rep + query_pos[..., :PE] * cos_sign
    turned_key = key_pos[..., PE:] * sin_rep + key_pos[..., :PE] * cos_sign
    feats_heads = jnp.broadcast_to(box_feats.astype(jnp.bfloat16), (row_count, HEADS, seq_len, PE))
    left_all = jnp.concatenate(
        [query_heads, turned_query.astype(jnp.bfloat16), feats_heads], axis=-1
    )
    right_all = jnp.concatenate([key_heads, feats_heads, turned_key.astype(jnp.bfloat16)], axis=-1)

    def row_forward(inputs):
        left_side, right_side, row_values, row_pages = inputs
        return attend_row(left_side, right_side, row_values, row_pages, score_scale)

    ctx_rows, total_rows = lax.map(row_forward, (left_all, right_all, value_heads, page_ids))
    ctx_low = from_heads(ctx_rows).astype(jnp.bfloat16)
    attn_out = jnp.dot(ctx_low, full_out, preferred_element_type=jnp.float32) + bias_out.astype(
        jnp.float32
    )
    first_sum = flat_rows.astype(jnp.float32) + attn_out
    hidden, norm_back_one = jax.vjp(
        layer_norm, first_sum, gain_first.astype(jnp.float32), shift_first.astype(jnp.float32)
    )
    hidden_low = hidden.astype(jnp.bfloat16)
    up_proj = jnp.dot(hidden_low, full_up, preferred_element_type=jnp.float32) + bias_up.astype(
        jnp.float32
    )
    activated, gelu_back = jax.vjp(gelu_exact, up_proj)
    act_low = activated.astype(jnp.bfloat16)
    ffn_out = jnp.dot(act_low, full_down, preferred_element_type=jnp.float32) + bias_down.astype(
        jnp.float32
    )
    result, norm_back_two = jax.vjp(
        layer_norm,
        hidden + ffn_out,
        gain_second.astype(jnp.float32),
        shift_second.astype(jnp.float32),
    )
    layer_out = result.reshape(row_count, seq_len, model_width).astype(jnp.bfloat16)
    again = (
        lax.all_gather(shards[0], "fsdp", axis=0, tiled=True),
        lax.all_gather(shards[1], "fsdp", axis=0, tiled=True),
        lax.all_gather(shards[2], "fsdp", axis=0, tiled=True),
        lax.all_gather(shards[3], "fsdp", axis=0, tiled=True),
        lax.all_gather(shards[4], "fsdp", axis=0, tiled=True),
        lax.all_gather(shards[5], "fsdp", axis=0, tiled=True),
        lax.all_gather(shards[6], "fsdp", axis=0, tiled=True),
        lax.all_gather(shards[7], "fsdp", axis=0, tiled=True),
        lax.all_gather(shards[8], "fsdp", axis=0, tiled=True),
        lax.all_gather(shards[9], "fsdp", axis=0, tiled=True),
        lax.all_gather(shards[10], "fsdp", axis=0, tiled=True),
        lax.all_gather(shards[11], "fsdp", axis=0, tiled=True),
        lax.all_gather(shards[12], "fsdp", axis=0, tiled=True),
    )
    back_qkv, back_out, back_up, back_down = (again[0], again[1], again[2], again[3])
    back_pos = again[5].reshape(2, PE, HD).astype(jnp.float32)
    back_comb_query = jnp.concatenate([back_pos[1], pair_swap(back_pos[1])], axis=0)
    back_comb_key = jnp.concatenate([back_pos[0], pair_swap(back_pos[0])], axis=0)
    grad_result = cotangent.reshape(tok_count, model_width).astype(jnp.float32)
    grad_second, grad_gain_two, grad_shift_two = norm_back_two(grad_result)
    grad_ffn = grad_second.astype(jnp.bfloat16)
    grad_w_down = jnp.einsum("nf,nd->fd", act_low, grad_ffn, preferred_element_type=jnp.float32)
    grad_b_down = jnp.sum(grad_ffn.astype(jnp.float32), axis=0)
    grad_act = jnp.einsum("nd,fd->nf", grad_ffn, back_down, preferred_element_type=jnp.float32)
    grad_up = gelu_back(grad_act)[0].astype(jnp.bfloat16)
    grad_w_up = jnp.einsum("nd,nf->df", hidden_low, grad_up, preferred_element_type=jnp.float32)
    grad_b_up = jnp.sum(grad_up.astype(jnp.float32), axis=0)
    grad_hidden = grad_second + jnp.einsum(
        "nf,df->nd", grad_up, back_up, preferred_element_type=jnp.float32
    )
    grad_first, grad_gain_one, grad_shift_one = norm_back_one(grad_hidden)
    grad_attn = grad_first.astype(jnp.bfloat16)
    grad_w_out = jnp.einsum("nc,nd->cd", ctx_low, grad_attn, preferred_element_type=jnp.float32)
    grad_b_out = jnp.sum(grad_attn.astype(jnp.float32), axis=0)
    grad_ctx = jnp.einsum(
        "nd,cd->nc", grad_attn, back_out, preferred_element_type=jnp.float32
    ).astype(jnp.bfloat16)

    def row_backward(inputs):
        left_side, right_side, row_values, row_pages, log_total, row_grad = inputs
        return attend_back(
            left_side, right_side, row_values, row_pages, log_total, row_grad, score_scale
        )

    grad_left, grad_right, grad_values = lax.map(
        row_backward, (left_all, right_all, value_heads, page_ids, total_rows, to_heads(grad_ctx))
    )
    grad_turn_query = grad_left[..., HD : HD + PE]
    grad_turn_key = grad_right[..., HD + PE :]
    grad_comb_q = jnp.concatenate([grad_turn_query * cos_sign, grad_turn_query * sin_rep], axis=-1)
    grad_comb_k = jnp.concatenate([grad_turn_key * cos_sign, grad_turn_key * sin_rep], axis=-1)
    grad_query = grad_left[..., :HD] + jnp.einsum(
        "rhlf,fd->rhld", grad_comb_q, back_comb_query, precision=lax.Precision.HIGHEST
    )
    grad_keys = grad_right[..., :HD] + jnp.einsum(
        "rhlf,fd->rhld", grad_comb_k, back_comb_key, precision=lax.Precision.HIGHEST
    )
    comb_from_query = jnp.einsum(
        "rhld,rhlf->fd",
        query_heads.astype(jnp.float32),
        grad_comb_q,
        precision=lax.Precision.HIGHEST,
    )
    comb_from_key = jnp.einsum(
        "rhld,rhlf->fd", key_heads.astype(jnp.float32), grad_comb_k, precision=lax.Precision.HIGHEST
    )
    grad_pos_key = comb_from_query[:PE] + pair_swap(comb_from_query[PE:])
    grad_pos_query = comb_from_key[:PE] + pair_swap(comb_from_key[PE:])
    grad_w_pos = jnp.stack([grad_pos_query, grad_pos_key]).reshape(2 * PE * HD)
    grad_qkv = jnp.concatenate(
        [from_heads(grad_query), from_heads(grad_keys), from_heads(grad_values)], axis=1
    ).astype(jnp.bfloat16)
    grad_w_qkv = jnp.einsum("nd,ne->de", flat_rows, grad_qkv, preferred_element_type=jnp.float32)
    grad_b_qkv = jnp.sum(grad_qkv.astype(jnp.float32), axis=0)
    grad_input = grad_first + jnp.einsum(
        "ne,de->nd", grad_qkv, back_qkv, preferred_element_type=jnp.float32
    )
    grad_tokens = grad_input.reshape(row_count, seq_len, model_width).astype(jnp.bfloat16)
    partials = (
        grad_w_qkv,
        grad_w_out,
        grad_w_up,
        grad_w_down,
        grad_b_qkv,
        grad_w_pos,
        grad_b_out,
        grad_gain_one,
        grad_shift_one,
        grad_b_up,
        grad_b_down,
        grad_gain_two,
        grad_shift_two,
    )
    shard_sums = (
        lax.psum_scatter(partials[0], "fsdp", scatter_dimension=0, tiled=True),
        lax.psum_scatter(partials[1], "fsdp", scatter_dimension=0, tiled=True),
        lax.psum_scatter(partials[2], "fsdp", scatter_dimension=0, tiled=True),
        lax.psum_scatter(partials[3], "fsdp", scatter_dimension=0, tiled=True),
        lax.psum_scatter(partials[4], "fsdp", scatter_dimension=0, tiled=True),
        lax.psum_scatter(partials[5], "fsdp", scatter_dimension=0, tiled=True),
        lax.psum_scatter(partials[6], "fsdp", scatter_dimension=0, tiled=True),
        lax.psum_scatter(partials[7], "fsdp", scatter_dimension=0, tiled=True),
        lax.psum_scatter(partials[8], "fsdp", scatter_dimension=0, tiled=True),
        lax.psum_scatter(partials[9], "fsdp", scatter_dimension=0, tiled=True),
        lax.psum_scatter(partials[10], "fsdp", scatter_dimension=0, tiled=True),
        lax.psum_scatter(partials[11], "fsdp", scatter_dimension=0, tiled=True),
        lax.psum_scatter(partials[12], "fsdp", scatter_dimension=0, tiled=True),
    )
    totals = (
        lax.psum(shard_sums[0].astype(jnp.bfloat16), "rep").astype(jnp.float32),
        lax.psum(shard_sums[1].astype(jnp.bfloat16), "rep").astype(jnp.float32),
        lax.psum(shard_sums[2].astype(jnp.bfloat16), "rep").astype(jnp.float32),
        lax.psum(shard_sums[3].astype(jnp.bfloat16), "rep").astype(jnp.float32),
        lax.psum(shard_sums[4].astype(jnp.bfloat16), "rep").astype(jnp.float32),
        lax.psum(shard_sums[5].astype(jnp.bfloat16), "rep").astype(jnp.float32),
        lax.psum(shard_sums[6].astype(jnp.bfloat16), "rep").astype(jnp.float32),
        lax.psum(shard_sums[7].astype(jnp.bfloat16), "rep").astype(jnp.float32),
        lax.psum(shard_sums[8].astype(jnp.bfloat16), "rep").astype(jnp.float32),
        lax.psum(shard_sums[9].astype(jnp.bfloat16), "rep").astype(jnp.float32),
        lax.psum(shard_sums[10].astype(jnp.bfloat16), "rep").astype(jnp.float32),
        lax.psum(shard_sums[11].astype(jnp.bfloat16), "rep").astype(jnp.float32),
        lax.psum(shard_sums[12].astype(jnp.bfloat16), "rep").astype(jnp.float32),
    )
    (
        sum_w_qkv,
        sum_w_out,
        sum_w_up,
        sum_w_down,
        sum_b_qkv,
        sum_w_pos,
        sum_b_out,
        sum_gain_one,
        sum_shift_one,
        sum_b_up,
        sum_b_down,
        sum_gain_two,
        sum_shift_two,
    ) = totals
    return (
        layer_out,
        grad_tokens,
        sum_w_qkv,
        sum_b_qkv,
        sum_w_pos,
        sum_w_out,
        sum_b_out,
        sum_gain_one,
        sum_shift_one,
        sum_w_up,
        sum_b_up,
        sum_w_down,
        sum_b_down,
        sum_gain_two,
        sum_shift_two,
    )


def solution(mesh):
    in_specs = (
        P(("fsdp", "rep"), None, None),
        P(("fsdp", "rep"), None),
        P(None, ("fsdp", "rep"), None),
        P("fsdp", None),
        P("fsdp"),
        P("fsdp"),
        P("fsdp", None),
        P("fsdp"),
        P("fsdp"),
        P("fsdp"),
        P("fsdp", None),
        P("fsdp"),
        P("fsdp", None),
        P("fsdp"),
        P("fsdp"),
        P("fsdp"),
        P(("fsdp", "rep"), None, None),
    )
    out_specs = (
        P(("fsdp", "rep"), None, None),
        P(("fsdp", "rep"), None, None),
        P("fsdp", None),
        P("fsdp"),
        P("fsdp"),
        P("fsdp", None),
        P("fsdp"),
        P("fsdp"),
        P("fsdp"),
        P("fsdp", None),
        P("fsdp"),
        P("fsdp", None),
        P("fsdp"),
        P("fsdp"),
        P("fsdp"),
    )
    return jax.shard_map(body, mesh=mesh, in_specs=in_specs, out_specs=out_specs, check_vma=False)
```

profile of v0, /device:TPU:0, one launch (start us, length us, event | category | flops | bytes accessed | tf_op | source)
XLA Modules:
  0.0 1125.1 jit_solution(646275522644799636)
XLA Ops:
  10.0 33.1 %all_gather.46 = bf16[24576]{0:T(1024)(128)(2,1)S(1)} all-gather(bf16[3072]{0:T(1024)(128)(2,1)} %param.26), channel_id=1, replica_groups=mesh['fsdp'=8,'rep'=4] {'fsdp'}, dimensions={0}, use_global_device_ids=true | all-gather | bytes 55296 | tf_op jit(solution)/shard_map/all_gather | solution.py:108
  53.1 38.1 %all-reduce.17 = (bf16[2304]{0:T(1024)(128)(2,1)S(1)}, bf16[768]{0:T(1024)(128)(2,1)S(1)}, bf16[768]{0:T(1024)(128)(2,1)S(1)}, bf16[768]{0:T(1024)(128)(2,1)S(1)...) all-reduce(bf16[2304]{0:T(1024)(128)(2,1)S(1)} %dynamic-update-slic, ...), channel_id=1, replica_groups=mesh['fsdp'=8,'rep'=4] {'fsdp'}, use_global_device_ids=true, to_apply=%add | all-reduce | flops 6912 | bytes 27648
  94.2 26.3 %all-gather = bf16[8,1,384]{2,1,0:T(2,128)(2,1)S(1)} all-gather(bf16[1,1,384]{2,1,0:T(2,128)(2,1)S(1)} %reshape.371), channel_id=1, replica_groups=mesh['fsdp'=8,'rep'=4] {'fsdp'}, dimensions={0}, use_global_device_ids=true | all-gather | bytes 6912 | tf_op jit(solution)/shard_map/all_gather | solution.py:112
  133.9 6.6 add_convert_fusion.1
  156.4 3.9 reshape.333
  160.3 4.4 copy_bitcast_fusion
  167.6 8.1 fusion.134
  175.7 13.3 %fusion.98 = (bf16[2,12,512,192]{2,3,1,0:T(8,128)(2,1)}, bf16[2,12,512,192]{2,3,1,0:T(8,128)(2,1)}) fusion(f32[2,12,512,384]{2,3,1,0:T(8,128)} %fusion.134, f32[2,512,192]{1,2,0:T(8,128)} %copy.174, f32[2,512,192]{1,2,0:T(8,128)} %copy.172, f32[2,12,512,384]{2,3,1,0:T(8,128)S(1)} %fusion.131), kind=kLoop, calls=%fused_computation.103 | loop fusion | flops 18874368 | bytes 48758784 | tf_op jit(solution)/shard_map/convert_element_type | solution.py:171
  191.4 11.2 pad_maximum_fusion.3
  203.8 50.8 %while.26 = (s32[]{:T(128)}, bf16[2,12,512,64]{2,3,1,0:T(8,128)(2,1)}, f32[2,12,512,1]{2,1,3,0:T(8,128)}, s32[2,512]{1,0:T(2,128)S(1)}, bf16[2,12,512,448]{2,3,1...) while((s32[]{:T(128)}, ...), condition=%wide.region_3.4_spmd, body=%wide.region_0.3_spmd.sunk | while | flops 3256084480 | bytes 102719608 | solution.py:177
  204.2 12.8 %fusion.195 = (f32[12,512]{1,0:T(8,128)S(1)}, f32[12,512,512]{1,2,0:T(8,128)}) fusion(pred[512,512]{0,1:T(8,128)(4,1)S(1)} %broadcast_compare_fusion.4, bf16[2,12,512,448]{2,3,1,0:T(8,128)(2,1)} %get-tuple-element.507, s32[]{:T(128)S(6)} %copy.269, bf16[2,12,512,448]{2,3,1,0:T(8,128)(2,1)} %get-tuple-element.506), kind=kOutput, calls=%fused_computation.3.clone.1 | convolution fusion | flops 2828003328 | bytes 23880704 | tf_op jit(solution)/shard_map/while/body/eval_jaxpr/hie,hje->hij/dot_general | solution.py:29
  217.0 7.3 exponential_reduce_fusion.2
  225.3 4.0 bitcast_dynamic-update-slice_fusion.11
  229.5 12.7 %fusion.195 = (f32[12,512]{1,0:T(8,128)S(1)}, f32[12,512,512]{1,2,0:T(8,128)}) fusion(pred[512,512]{0,1:T(8,128)(4,1)S(1)} %broadcast_compare_fusion.4, bf16[2,12,512,448]{2,3,1,0:T(8,128)(2,1)} %get-tuple-element.507, s32[]{:T(128)S(6)} %copy.269, bf16[2,12,512,448]{2,3,1,0:T(8,128)(2,1)} %get-tuple-element.506), kind=kOutput, calls=%fused_computation.3.clone.1 | convolution fusion | flops 2828003328 | bytes 23880704 | tf_op jit(solution)/shard_map/while/body/eval_jaxpr/hie,hje->hij/dot_general | solution.py:29
  242.2 7.3 exponential_reduce_fusion.2
  250.5 4.0 bitcast_dynamic-update-slice_fusion.11
  259.9 3.9 fusion.154
  264.4 36.4 %multiply_convert_fusion.1 = (bf16[1024,3072]{1,0:T(8,128)(2,1)}, f32[1024,3072]{1,0:T(8,128)}, f32[1024,3072]{1,0:T(8,128)}) fusion(f32[3072]{0:T(1024)S(1)} %bitcast.258, bf16[768,3072]{1,0:T(8,128)(2,1)} %all-gather.10.cloned.1.call-done, f32[1024,768]{1,0:T(8,128)S(1)} %get-tuple-element.363, f32[768]{0:T(1024)S(1)} %copy-done.37, ...), kind=kOutput, calls=%fused_computation.85 | convolution fusion | flops 5043388416 | bytes 39348224 | tf_op jit(solution)/shard_map/dot_general | solution.py:187
  300.8 9.4 fusion.155
  317.2 19.0 %convert_reduce_fusion = (f32[3072]{0:T(1024)}, bf16[1024,3072]{1,0:T(8,128)(2,1)}) fusion(f32[1024,3072]{1,0:T(8,128)} %get-tuple-element.334, bf16[1024,768]{1,0:T(8,128)(2,1)} %get-tuple-element.326, bf16[3072,768]{1,0:T(8,128)(2,1)} %all-gather.12.cloned.1.call-done, f32[1024,3072]{1,0:T(8,128)} %get-tuple-element.364, f32[3072]{0:T(1024)S(1)} %bitcast.259), kind=kOutput, calls=%fused_computation.83 | convolution fusion | flops 4885312512 | bytes 37773312 | tf_op jit(solution)/shard_map/nd,fd->nf/dot_general | solution.py:226
  336.2 10.1 multiply_reduce_fusion.1
  363.1 155.6 %while.27 = (s32[]{:T(128)}, f32[2,12,512,448]{2,3,1,0:T(8,128)}, f32[2,12,512,448]{2,3,1,0:T(8,128)}, bf16[2,12,512,64]{2,3,1,0:T(8,128)(2,1)}, s32[2,512]{1,0:...) while((s32[]{:T(128)}, f32[2,12,512,448]{2,3,1,0:T(8,128)}, ...), condition=%wide.region_14.15_spmd, body=%wide.region_12.14_spmd.sunk | while | flops 9343087616 | bytes 188181648 | solution.py:247
  363.5 12.4 %fusion.207 = f32[12,512,512]{1,2,0:T(8,128)} fusion(bf16[2,12,512,448]{2,3,1,0:T(8,128)(2,1)} %get-tuple-element.538, s32[]{:T(128)S(6)} %copy.279, bf16[2,12,512,448]{2,3,1,0:T(8,128)(2,1)} %get-tuple-element.537), kind=kOutput, calls=%fused_computation.43.clone.1 | convolution fusion | flops 2818572288 | bytes 23593984 | tf_op jit(solution)/shard_map/while/body/eval_jaxpr/hie,hje->hij/dot_general | solution.py:29
  376.0 7.4 bitcast_dynamic-update-slice_fusion.14
  383.4 6.3 fusion.206
  389.7 27.8 %bitcast_dynamic-update-slice_fusion.13 = f32[2,12,512,448]{2,3,1,0:T(8,128)} fusion(f32[2,12,512,448]{2,3,1,0:T(8,128)} %get-tuple-element.523, s32[]{:T(128)S(6)} %copy.279, bf16[2,12,512,448]{2,3,1,0:T(8,128)(2,1)} %get-tuple-element.537, f32[12,512,512]{1,2,0:T(8,128)} %fusion.206, f32[12,512,512]{1,2,0:T(8,128)} %fusion.207, ...), kind=kOutput, calls=%fused_computation.27.clone.1 | convolution fusion | flops 2853181952 | bytes 67437568 | tf_op jit(solution)/shard_map/while/body/eval_jaxpr/hij,hie->hje/dot_general | solution.py:56
  417.5 23.7 %bitcast_dynamic-update-slice_fusion.12 = f32[2,12,512,448]{2,3,1,0:T(8,128)} fusion(f32[2,12,512,448]{2,3,1,0:T(8,128)} %get-tuple-element.522, s32[]{:T(128)S(6)} %copy.279, f32[12,512,512]{1,2,0:T(8,128)} %fusion.206, f32[12,512,512]{1,2,0:T(8,128)} %fusion.207, f32[12,512]{1,0:T(8,128)S(1)} %dynamic-slice_bitcast_fusion.2, ...), kind=kOutput, calls=%fused_computation.28.clone.1 | convolution fusion | flops 2853181952 | bytes 67437568 | tf_op jit(solution)/shard_map/while/body/eval_jaxpr/hij,hje->hie/dot_general | solution.py:53
  441.4 12.2 %fusion.207 = f32[12,512,512]{1,2,0:T(8,128)} fusion(bf16[2,12,512,448]{2,3,1,0:T(8,128)(2,1)} %get-tuple-element.538, s32[]{:T(128)S(6)} %copy.279, bf16[2,12,512,448]{2,3,1,0:T(8,128)(2,1)} %get-tuple-element.537), kind=kOutput, calls=%fused_computation.43.clone.1 | convolution fusion | flops 2818572288 | bytes 23593984 | tf_op jit(solution)/shard_map/while/body/eval_jaxpr/hie,hje->hij/dot_general | solution.py:29
  453.6 7.2 bitcast_dynamic-update-slice_fusion.14
  460.8 6.3 fusion.206
  467.2 27.8 %bitcast_dynamic-update-slice_fusion.13 = f32[2,12,512,448]{2,3,1,0:T(8,128)} fusion(f32[2,12,512,448]{2,3,1,0:T(8,128)} %get-tuple-element.523, s32[]{:T(128)S(6)} %copy.279, bf16[2,12,512,448]{2,3,1,0:T(8,128)(2,1)} %get-tuple-element.537, f32[12,512,512]{1,2,0:T(8,128)} %fusion.206, f32[12,512,512]{1,2,0:T(8,128)} %fusion.207, ...), kind=kOutput, calls=%fused_computation.27.clone.1 | convolution fusion | flops 2853181952 | bytes 67437568 | tf_op jit(solution)/shard_map/while/body/eval_jaxpr/hij,hie->hje/dot_general | solution.py:56
  494.9 23.6 %bitcast_dynamic-update-slice_fusion.12 = f32[2,12,512,448]{2,3,1,0:T(8,128)} fusion(f32[2,12,512,448]{2,3,1,0:T(8,128)} %get-tuple-element.522, s32[]{:T(128)S(6)} %copy.279, f32[12,512,512]{1,2,0:T(8,128)} %fusion.206, f32[12,512,512]{1,2,0:T(8,128)} %fusion.207, f32[12,512]{1,0:T(8,128)S(1)} %dynamic-slice_bitcast_fusion.2, ...), kind=kOutput, calls=%fused_computation.28.clone.1 | convolution fusion | flops 2853181952 | bytes 67437568 | tf_op jit(solution)/shard_map/while/body/eval_jaxpr/hij,hje->hie/dot_general | solution.py:53
  522.3 18.4 %slice_multiply_fusion.7 = (f32[2,12,512,192]{2,3,1,0:T(8,128)}, f32[2,12,512,192]{2,3,1,0:T(8,128)}, f32[2,12,512,192]{2,3,1,0:T(8,128)S(1)}, f32[2,12,512,192]{2,3,1,0:T(8,128)}) fusion(f32[2,12,512,448]{2,3,1,0:T(8,128)} %get-tuple-element.109, f32[2,512,192]{1,2,0:T(8,128)S(1)} %copy-done.17, f32[2,512,192]{1,2,0:T(8,128)S(1)} %copy-done.16, ...), kind=kLoop, calls=%fused_computation.114 | loop fusion | flops 9437184 | bytes 58195968 | tf_op jit(solution)/shard_map/mul | solution.py:252
  540.7 19.8 %fusion.110 = bf16[2,512,12,64]{1,3,2,0:T(8,128)(2,1)S(1)} fusion(f32[2,12,512,448]{2,3,1,0:T(8,128)} %get-tuple-element.109, f32[192,64]{0,1:T(8,128)S(1)} %copy-done.27, f32[192,64]{0,1:T(8,128)S(1)} %copy-done.28, f32[2,12,512,192]{2,3,1,0:T(8,128)} %get-tuple-element.340, f32[2,12,512,192]{2,3,1,0:T(8,128)} %get-tuple-element.339), kind=kOutput, calls=%fused_computation.151 | convolution fusion | flops 3630194688 | bytes 23691264 | tf_op jit(solution)/shard_map/rhlf,fd->rhld/dot_general | solution.py:254
  562.6 15.7 %fusion.111 = bf16[2,512,12,64]{1,3,2,0:T(8,128)(2,1)} fusion(f32[2,12,512,448]{2,3,1,0:T(8,128)} %get-tuple-element.110, f32[192,64]{0,1:T(8,128)S(1)} %copy-done.25, f32[192,64]{0,1:T(8,128)S(1)} %copy-done.26, f32[2,12,512,192]{2,3,1,0:T(8,128)S(1)} %get-tuple-element.347, f32[2,12,512,192]{2,3,1,0:T(8,128)} %get-tuple-element.348), kind=kOutput, calls=%fused_computation.152 | convolution fusion | flops 3630194688 | bytes 23691264 | tf_op jit(solution)/shard_map/rhlf,fd->rhld/dot_general | solution.py:257
  584.3 5.8 convolution_bitcast_fusion
  590.1 8.1 copy.224
  600.1 11.3 %fusion.143 = f32[768,3072]{1,0:T(8,128)} fusion(bf16[1024,3072]{1,0:T(8,128)(2,1)} %get-tuple-element.369, f32[1024,768]{1,0:T(8,128)S(1)} %copy-done.3, f32[768]{0:T(1024)S(1)} %copy-done.38, f32[768]{0:T(1024)S(1)} %copy-done.34, f32[1024]{0:T(1024)S(1)} %copy-done.24, f32[1024]{0:T(1024)S(1)} %copy-done.22), kind=kOutput, calls=%fused_computation.210 | convolution fusion | flops 4835770368 | bytes 18888704 | tf_op jit(solution)/shard_map/nd,nf->df/dot_general | solution.py:228
  612.8 10.4 fusion.157
  626.4 13.3 %fusion.117 = f32[384,64]{0,1:T(8,128)S(1)} fusion(bf16[2,512,12,64]{1,0,3,2:T(2,128)(2,1)S(1)} %copy-done.10, f32[2,12,512,192]{2,3,1,0:T(8,128)} %get-tuple-element.340, f32[2,12,512,192]{2,3,1,0:T(8,128)} %get-tuple-element.339), kind=kOutput, calls=%fused_computation.154 | convolution fusion | flops 3628597248 | bytes 20545536 | tf_op jit(solution)/shard_map/rhld,rhlf->fd/dot_general | solution.py:260
  640.3 13.0 %fusion.112 = f32[384,64]{0,1:T(8,128)S(1)} fusion(bf16[2,512,12,64]{1,0,3,2:T(2,128)(2,1)S(1)} %copy-done.8, f32[2,12,512,192]{2,3,1,0:T(8,128)} %copy-done.1, f32[2,12,512,192]{2,3,1,0:T(8,128)} %get-tuple-element.348), kind=kOutput, calls=%fused_computation.153 | convolution fusion | flops 3628597248 | bytes 20545536 | tf_op jit(solution)/shard_map/rhld,rhlf->fd/dot_general | solution.py:266
  657.4 35.1 %all-reduce.24 = (bf16[2304]{0:T(1024)(128)(2,1)S(1)}, bf16[24576]{0:T(1024)(128)(2,1)S(1)}, bf16[768]{0:T(1024)(128)(2,1)S(1)}, bf16[768]{0:T(1024)(128)(2,1)S(...) all-reduce(f32[2304]{0:T(1024)S(1)} %convert_reduce_fusion.1, ...), channel_id=3, replica_groups=mesh['fsdp'=8,'rep'=4] {'fsdp'}, use_global_device_ids=true, to_apply=%region_18.19.clone | all-reduce | flops 34560 | bytes 207360
  693.1 10.7 all-reduce.18
  710.3 18.5 %reduce-scatter.13.cloned.1.call-done = f32[96,2304]{1,0:T(8,128)} async-done(((f32[768,2304]{1,0:T(8,128)}), f32[96,2304]{1,0:T(8,128)}) %reduce-scatter.13.cloned.1.call-update) | async-done | bytes 884752
  731.0 162.6 %reduce-scatter.9.cloned.1.call-done = f32[96,3072]{1,0:T(8,128)} async-done(((f32[768,3072]{1,0:T(8,128)}), f32[96,3072]{1,0:T(8,128)}) %reduce-scatter.9.cloned.1.call-update) | async-done | bytes 1179664 | tf_op jit(solution)/shard_map/reduce_scatter | solution.py:299
  895.8 162.7 %reduce-scatter.11.cloned.1.call-done = f32[384,768]{1,0:T(8,128)} async-done(((f32[3072,768]{1,0:T(8,128)}), f32[384,768]{1,0:T(8,128)}) %reduce-scatter.11.cloned.1.call-update) | async-done | bytes 1179664 | tf_op jit(solution)/shard_map/reduce_scatter | solution.py:300
  1060.7 8.6 add_convert_fusion.2
  1069.3 40.8 %all-reduce.23.cloned.1.call-done = (bf16[96,2304]{0,1:T(8,128)(2,1)}, bf16[96,768]{1,0:T(8,128)(2,1)}, bf16[96,3072]{1,0:T(8,128)(2,1)}, bf16[384,768]{1,0:T(8,128)(2,1)}) async-done(((bf16[96,2304]{0,1:T(8,128)(2,1)}, bf16[96,768]{1,0:T(8,128)(2,1)}, bf16[96,3072]{1,0:T(8,128)(2,1)}, bf16[384,768]{1,0:T(8,128)(2,1)}), (bf16[96,2304]{0,1:T(8,128)(2,1)}, bf16[96,768]{1,0:T(8,128)(2,1)}, ...) | async-done | bytes 1769488 | tf_op jit(solution)/shard_map/psum | solution.py:312
  (289 shorter events, 123.6 us)
Async XLA Ops:
  7.2 126.7 %all-gather.6.cloned.1.call-start = ((), (), s32[]{:S(2)}) async-start(), calls=%async_computation.4 | async-start | bytes 3981312 | tf_op jit(solution)/shard_map/all_gather | solution.py:103
  7.9 252.0 %all-gather.8.cloned.1.call-start = ((), (), s32[]{:S(2)}) async-start(), calls=%async_computation.5 | async-start | bytes 1327104 | tf_op jit(solution)/shard_map/all_gather | solution.py:104
  8.7 255.6 %all-gather.10.cloned.1.call-start = ((), (), s32[]{:S(2)}) async-start(), calls=%async_computation.6 | async-start | bytes 5308416 | tf_op jit(solution)/shard_map/all_gather | solution.py:105
  9.4 291.4 %all-gather.12.cloned.1.call-start = ((), (), s32[]{:S(2)}) async-start(), calls=%async_computation.7 | async-start | bytes 5308416 | tf_op jit(solution)/shard_map/all_gather | solution.py:106
  10.0 698.7 %reduce-scatter.7.cloned.1.call-start = ((), (), s32[]{:S(2)}) async-start(), calls=%async_computation.8 | async-start | bytes 2654208 | tf_op jit(solution)/shard_map/reduce_scatter | solution.py:298
  128.4 5.5 copy-start.51
  153.8 10.9 copy-start.31
  153.8 10.9 copy-start.32
  160.3 4.4 copy-start.9
  191.4 12.5 %copy-start.35 = (s32[2,512]{1,0:T(2,128)S(1)}, s32[2,512]{1,0:T(2,128)}, u32[]{:S(2)}) copy-start(s32[2,512]{1,0:T(2,128)} %param.22) | copy-start | bytes 12292
  217.0 8.3 copy-start
  242.2 8.3 copy-start
  254.7 5.2 copy-start.4
  259.9 4.4 copy-start.33
  259.9 4.5 copy-start.37
  259.9 4.5 copy-start.47
  263.8 82.6 %copy-start.2 = (f32[1024,768]{1,0:T(8,128)}, f32[1024,768]{1,0:T(8,128)S(1)}, u32[]{:S(2)}) copy-start(f32[1024,768]{1,0:T(8,128)S(1)} %get-tuple-element.363) | copy-start | bytes 9437188
  263.8 82.6 %copy-start.21 = (f32[1024]{0:T(1024)}, f32[1024]{0:T(1024)S(1)}, u32[]{:S(2)}) copy-start(f32[1024]{0:T(1024)S(1)} %broadcast_multiply_fusion.1) | copy-start | bytes 12292
  264.3 82.1 %copy-start.23 = (f32[1024]{0:T(1024)}, f32[1024]{0:T(1024)S(1)}, u32[]{:S(2)}) copy-start(f32[1024]{0:T(1024)S(1)} %fusion.137) | copy-start | bytes 12292
  264.3 36.4 %copy-start.50 = (f32[768]{0:T(1024)S(1)}, f32[768]{0:T(1024)}, u32[]{:S(2)}) copy-start(f32[768]{0:T(1024)} %convert_element_type.230) | copy-start | bytes 9220
  300.8 10.0 copy-start.11
  300.8 10.0 copy-start.39
  346.3 4.0 copy-start.18
  347.8 5.4 copy-start.53
  355.8 7.3 copy-start.5
  355.8 7.3 copy-start.20
  355.8 7.3 copy-start.36
  361.7 367.1 %reduce-scatter.13.cloned.1.call-start = ((), (), s32[]{:S(2)}) async-start(), calls=%async_computation.11 | async-start | bytes 7962624
  518.7 3.6 copy-start.16
  518.7 3.6 copy-start.17
  522.3 18.4 %copy-start.27 = (f32[192,64]{0,1:T(8,128)S(1)}, f32[192,64]{0,1:T(8,128)}, u32[]{:S(2)}) copy-start(f32[192,64]{0,1:T(8,128)} %copy.188) | copy-start | bytes 147460
  522.3 18.4 %copy-start.28 = (f32[192,64]{0,1:T(8,128)S(1)}, f32[192,64]{0,1:T(8,128)}, u32[]{:S(2)}) copy-start(f32[192,64]{0,1:T(8,128)} %copy.187) | copy-start | bytes 147460
  540.7 21.9 %copy-start.1 = (f32[2,12,512,192]{2,3,1,0:T(8,128)}, f32[2,12,512,192]{2,3,1,0:T(8,128)S(1)}, u32[]{:S(2)}) copy-start(f32[2,12,512,192]{2,3,1,0:T(8,128)S(1)} %get-tuple-element.347) | copy-start | bytes 28311556
  581.4 3.0 copy-start.52
  598.3 295.4 %reduce-scatter.9.cloned.1.call-start = ((), (), s32[]{:S(2)}) async-start(), calls=%async_computation.9 | async-start | bytes 10616832 | tf_op jit(solution)/shard_map/reduce_scatter | solution.py:299
  611.4 447.1 %reduce-scatter.11.cloned.1.call-start = ((), (), s32[]{:S(2)}) async-start(), calls=%async_computation.10 | async-start | bytes 10616832 | tf_op jit(solution)/shard_map/reduce_scatter | solution.py:300
  623.2 2.9 copy-start.12
  623.2 3.2 copy-start.10
  623.2 486.9 %all-reduce.23.cloned.1.call-start = ((), (), s32[]{:S(2)}) async-start(), calls=%async_computation.12 | async-start | bytes 3833856 | tf_op jit(solution)/shard_map/psum | solution.py:312
  626.4 13.8 %copy-start.8 = (bf16[2,512,12,64]{1,0,3,2:T(2,128)(2,1)S(1)}, bf16[2,512,12,64]{1,0,3,2:T(2,128)(2,1)}, u32[]{:S(2)}) copy-start(bf16[2,512,12,64]{1,0,3,2:T(2,128)(2,1)} %reshape.335) | copy-start | bytes 4718596
  653.3 4.1 copy-start.40
  653.3 4.1 copy-start.41
  653.3 4.1 copy-start.45
  653.3 4.1 copy-start.46
  653.3 4.1 copy-start.48
  653.4 4.1 copy-start.49
  654.0 406.7 %copy-start.14 = (f32[1024,768]{1,0:T(8,128)S(1)}, f32[1024,768]{1,0:T(8,128)}, u32[]{:S(2)}) copy-start(f32[1024,768]{1,0:T(8,128)} %copy-done.13) | copy-start | bytes 9437188
  654.0 406.7 %copy-start.43 = (f32[1024]{0:T(1024)S(1)}, f32[1024]{0:T(1024)}, u32[]{:S(2)}) copy-start(f32[1024]{0:T(1024)} %copy-done.42) | copy-start | bytes 12292
  (16 other events, 34.6 us)
Sparse Core Ops, SparseCore 0:
  10.2 68.5 all-gather.5
  81.0 39.8 all-gather.7
  123.0 78.0 all-gather.9
  203.1 77.6 all-gather.11
  361.9 66.4 reduce-scatter.6
  598.4 130.3 reduce-scatter.12
  732.4 161.2 reduce-scatter.8
  897.3 161.2 reduce-scatter.10
  1062.3 47.7 all-reduce.22
where the time goes:
time: 1130 us
  matrix products  388 us (34%)
  waiting for transfers between devices  387 us (34%)
  blocking collectives  143 us (13%)
  other arithmetic  95.8 us (8%)
  local copies, waits for them, and re-layouts  90.4 us (8%)
  between operations  19.3 us (2%)
    reduce_scatter x1, waiting for transfers between devices, body(): lax.psum_scatter(partials[3], 'fsdp', scatter_dimension=0, tiled=True)  163 us
    reduce_scatter x1, waiting for transfers between devices, body(): lax.psum_scatter(partials[2], 'fsdp', scatter_dimension=0, tiled=True)  163 us
    unnamed x2, blocking collectives  73.2 us
    dot_general x2, matrix products, attend_back(): jnp.einsum('hij,hie->hje', grad_logits, left_side, preferred_element_type...  55.5 us
    dot_general x4, matrix products, row_scores(): jnp.einsum('hie,hje->hij', left_side, right_side, preferred_element_type=...  50.1 us
    dot_general x2, matrix products, attend_back(): jnp.einsum('hij,hje->hie', grad_logits, right_side, preferred_element_typ...  47.3 us
    psum x1, waiting for transfers between devices, body(): lax.psum(shard_sums[0].astype(jnp.bfloat16), 'rep').astype(jnp.float32)  40.8 us
    dot_general x1, matrix products, body(): jnp.dot(hidden_low, full_up, preferred_element_type=jnp.float32)  36.4 us
  transfers between devices with their start and end apart: 9, of which 4 were waited for; matrix products, arithmetic and copies ran while one was open for 44% of the time, Pallas kernels for 0%

commit v1 on v0

--- a/solution.py
+++ b/solution.py
@@ -309,7 +309,9 @@
         lax.psum_scatter(partials[12], "fsdp", scatter_dimension=0, tiled=True),
     )
     totals = (
-        lax.psum(shard_sums[0].astype(jnp.bfloat16), "rep").astype(jnp.float32),
+        jnp.sum(lax.all_gather(shard_sums[0].astype(jnp.bfloat16), "rep"), axis=0).astype(
+            jnp.float32
+        ),
         lax.psum(shard_sums[1].astype(jnp.bfloat16), "rep").astype(jnp.float32),
         lax.psum(shard_sums[2].astype(jnp.bfloat16), "rep").astype(jnp.float32),
         lax.psum(shard_sums[3].astype(jnp.bfloat16), "rep").astype(jnp.float32),

time: 1130 us -> 1200 us (1.062)
  waiting for transfers between devices: 387 us -> 460 us
    reduce_scatter x0 -> x1, waiting for transfers between devices: none -> 98.3 us  [body(): lax.psum_scatter(partials[0], 'fsdp', scatter_dimension=0, tiled=True)]
    unnamed x10, waiting for transfers between devices: 21.2 us -> 2.68 us
    reduce_scatter x1, waiting for transfers between devices: 163 us -> 145 us  [body(): lax.psum_scatter(partials[2], 'fsdp', scatter_dimension=0, tiled=True)]
  transfers between devices with their start and end apart: 9 -> 10, of which waited for: 4 -> 5; matrix products, arithmetic and copies ran while one was open for 44% -> 22% of each run, Pallas kernels for 0% -> 0%
where the time goes in v1:
time: 1200 us
  waiting for transfers between devices  460 us (38%)
  matrix products  387 us (32%)
  blocking collectives  146 us (12%)
  other arithmetic  101 us (8%)
  local copies, waits for them, and re-layouts  79.9 us (7%)
  between operations  19.4 us (2%)
    reduce_scatter x1, waiting for transfers between devices, body(): lax.psum_scatter(partials[3], 'fsdp', scatter_dimension=0, tiled=True)  163 us
    reduce_scatter x1, waiting for transfers between devices, body(): lax.psum_scatter(partials[2], 'fsdp', scatter_dimension=0, tiled=True)  145 us
    reduce_scatter x1, waiting for transfers between devices, body(): lax.psum_scatter(partials[0], 'fsdp', scatter_dimension=0, tiled=True)  98.3 us
    unnamed x2, blocking collectives  76.1 us
    dot_general x2, matrix products, attend_back(): jnp.einsum('hij,hie->hje', grad_logits, left_side, preferred_element_type...  55.4 us
    dot_general x4, matrix products, row_scores(): jnp.einsum('hie,hje->hij', left_side, right_side, preferred_element_type=...  50.2 us
    dot_general x2, matrix products, attend_back(): jnp.einsum('hij,hje->hie', grad_logits, right_side, preferred_element_typ...  47.1 us
    psum x1, waiting for transfers between devices, body(): lax.psum(shard_sums[1].astype(jnp.bfloat16), 'rep').astype(jnp.float32)  40.4 us
  transfers between devices with their start and end apart: 10, of which 5 were waited for; matrix products, arithmetic and copies ran while one was open for 22% of the time, Pallas kernels for 0%

profile of v1, /device:TPU:0, one launch (start us, length us, event | category | flops | bytes accessed | tf_op | source)
XLA Modules:
  0.0 1196.2 jit_solution(13475859734327032279)
XLA Ops:
  10.0 33.1 %all_gather.52 = bf16[24576]{0:T(1024)(128)(2,1)S(1)} all-gather(bf16[3072]{0:T(1024)(128)(2,1)} %param.26), channel_id=1, replica_groups=mesh['fsdp'=8,'rep'=4] {'fsdp'}, dimensions={0}, use_global_device_ids=true | all-gather | bytes 55296 | tf_op jit(solution)/shard_map/all_gather | solution.py:108
  52.4 38.1 %all-reduce.17 = (bf16[2304]{0:T(1024)(128)(2,1)S(1)}, bf16[768]{0:T(1024)(128)(2,1)S(1)}, bf16[768]{0:T(1024)(128)(2,1)S(1)}, bf16[768]{0:T(1024)(128)(2,1)S(1)...) all-reduce(bf16[2304]{0:T(1024)(128)(2,1)S(1)} %dynamic-update-slic, ...), channel_id=1, replica_groups=mesh['fsdp'=8,'rep'=4] {'fsdp'}, use_global_device_ids=true, to_apply=%add | all-reduce | flops 6912 | bytes 27648
  100.1 26.5 %all-gather.1 = bf16[8,1,384]{2,1,0:T(2,128)(2,1)S(1)} all-gather(bf16[1,1,384]{2,1,0:T(2,128)(2,1)S(1)} %reshape.372), channel_id=1, replica_groups=mesh['fsdp'=8,'rep'=4] {'fsdp'}, dimensions={0}, use_global_device_ids=true | all-gather | bytes 6912 | tf_op jit(solution)/shard_map/all_gather | solution.py:112
  132.3 6.1 add_convert_fusion.1
  156.7 4.8 copy_bitcast_fusion
  164.4 8.1 fusion.134
  172.5 13.4 %fusion.98 = (bf16[2,12,512,192]{2,3,1,0:T(8,128)(2,1)}, bf16[2,12,512,192]{2,3,1,0:T(8,128)(2,1)}) fusion(f32[2,12,512,384]{2,3,1,0:T(8,128)} %fusion.134, f32[2,512,192]{1,2,0:T(8,128)} %copy.173, f32[2,512,192]{1,2,0:T(8,128)} %copy.171, f32[2,12,512,384]{2,3,1,0:T(8,128)S(1)} %fusion.131), kind=kLoop, calls=%fused_computation.103 | loop fusion | flops 18874368 | bytes 48758784 | tf_op jit(solution)/shard_map/convert_element_type | solution.py:171
  188.3 11.2 pad_maximum_fusion.3
  200.8 51.4 %while.26 = (s32[]{:T(128)}, bf16[2,12,512,64]{2,3,1,0:T(8,128)(2,1)}, f32[2,12,512,1]{2,1,3,0:T(8,128)}, s32[2,512]{1,0:T(2,128)S(1)}, bf16[2,12,512,448]{2,3,1...) while((s32[]{:T(128)}, ...), condition=%wide.region_3.4_spmd, body=%wide.region_0.3_spmd.sunk | while | flops 3256084480 | bytes 102720120 | solution.py:177
  201.5 12.7 %fusion.195 = (f32[12,512]{1,0:T(8,128)S(1)}, f32[12,512,512]{1,2,0:T(8,128)}) fusion(pred[512,512]{0,1:T(8,128)(4,1)S(1)} %broadcast_compare_fusion.4, bf16[2,12,512,448]{2,3,1,0:T(8,128)(2,1)} %get-tuple-element.431, s32[]{:T(128)} %get-tuple-element.418, bf16[2,12,512,448]{2,3,1,0:T(8,128)(2,1)} %get-tuple-element.430), kind=kOutput, calls=%fused_computation.3.clone.1 | convolution fusion | flops 2828003328 | bytes 23880704 | tf_op jit(solution)/shard_map/while/body/eval_jaxpr/hie,hje->hij/dot_general | solution.py:29
  214.3 7.3 exponential_reduce_fusion.2
  222.5 4.0 bitcast_dynamic-update-slice_fusion.11
  226.8 13.0 %fusion.195 = (f32[12,512]{1,0:T(8,128)S(1)}, f32[12,512,512]{1,2,0:T(8,128)}) fusion(pred[512,512]{0,1:T(8,128)(4,1)S(1)} %broadcast_compare_fusion.4, bf16[2,12,512,448]{2,3,1,0:T(8,128)(2,1)} %get-tuple-element.431, s32[]{:T(128)} %get-tuple-element.418, bf16[2,12,512,448]{2,3,1,0:T(8,128)(2,1)} %get-tuple-element.430), kind=kOutput, calls=%fused_computation.3.clone.1 | convolution fusion | flops 2828003328 | bytes 23880704 | tf_op jit(solution)/shard_map/while/body/eval_jaxpr/hie,hje->hij/dot_general | solution.py:29
  239.8 7.3 exponential_reduce_fusion.2
  248.0 4.0 bitcast_dynamic-update-slice_fusion.11
  261.8 36.2 %multiply_convert_fusion.1 = (bf16[1024,3072]{1,0:T(8,128)(2,1)}, f32[1024,3072]{1,0:T(8,128)}, f32[1024,3072]{1,0:T(8,128)}) fusion(f32[3072]{0:T(1024)S(1)} %bitcast.261, bf16[768,3072]{1,0:T(8,128)(2,1)} %all-gather.12.cloned.1.call-done, f32[1024,768]{1,0:T(8,128)S(1)} %get-tuple-element.287, f32[768]{0:T(1024)S(1)} %convert_element_type.228, ...), kind=kOutput, calls=%fused_computation.85 | convolution fusion | flops 5043388416 | bytes 39348224 | tf_op jit(solution)/shard_map/dot_general | solution.py:187
  298.1 9.1 fusion.155
  314.2 18.9 %convert_reduce_fusion = (f32[3072]{0:T(1024)}, bf16[1024,3072]{1,0:T(8,128)(2,1)}) fusion(f32[1024,3072]{1,0:T(8,128)} %get-tuple-element.258, bf16[1024,768]{1,0:T(8,128)(2,1)} %get-tuple-element.250, bf16[3072,768]{1,0:T(8,128)(2,1)} %all-gather.14.cloned.1.call-done, f32[1024,3072]{1,0:T(8,128)} %get-tuple-element.288, f32[3072]{0:T(1024)S(1)} %bitcast.262), kind=kOutput, calls=%fused_computation.83 | convolution fusion | flops 4885312512 | bytes 37773312 | tf_op jit(solution)/shard_map/nd,fd->nf/dot_general | solution.py:226
  333.1 10.1 multiply_reduce_fusion.1
  357.1 155.1 %while.27 = (s32[]{:T(128)}, f32[2,12,512,448]{2,3,1,0:T(8,128)}, f32[2,12,512,448]{2,3,1,0:T(8,128)}, bf16[2,12,512,64]{2,3,1,0:T(8,128)(2,1)}, s32[2,512]{1,0:...) while((s32[]{:T(128)}, f32[2,12,512,448]{2,3,1,0:T(8,128)}, ...), condition=%wide.region_14.15_spmd, body=%wide.region_12.14_spmd.sunk | while | flops 9343087616 | bytes 188181616 | solution.py:247
  357.6 12.2 %fusion.207 = f32[12,512,512]{1,2,0:T(8,128)} fusion(bf16[2,12,512,448]{2,3,1,0:T(8,128)(2,1)} %get-tuple-element.462, s32[]{:T(128)} %get-tuple-element.445, bf16[2,12,512,448]{2,3,1,0:T(8,128)(2,1)} %get-tuple-element.461), kind=kOutput, calls=%fused_computation.43.clone.1 | convolution fusion | flops 2818572288 | bytes 23593984 | tf_op jit(solution)/shard_map/while/body/eval_jaxpr/hie,hje->hij/dot_general | solution.py:29
  369.7 6.3 fusion.206
  376.3 27.7 %bitcast_dynamic-update-slice_fusion.13 = f32[2,12,512,448]{2,3,1,0:T(8,128)} fusion(f32[2,12,512,448]{2,3,1,0:T(8,128)} %get-tuple-element.447, s32[]{:T(128)} %get-tuple-element.445, bf16[2,12,512,448]{2,3,1,0:T(8,128)(2,1)} %get-tuple-element.461, f32[12,512,512]{1,2,0:T(8,128)} %fusion.206, f32[12,512,512]{1,2,0:T(8,128)} %fusion.207, ...), kind=kOutput, calls=%fused_computation.27.clone.1 | convolution fusion | flops 2853181952 | bytes 67437568 | tf_op jit(solution)/shard_map/while/body/eval_jaxpr/hij,hie->hje/dot_general | solution.py:56
  404.0 23.6 %bitcast_dynamic-update-slice_fusion.12 = f32[2,12,512,448]{2,3,1,0:T(8,128)} fusion(f32[2,12,512,448]{2,3,1,0:T(8,128)} %get-tuple-element.446, s32[]{:T(128)} %get-tuple-element.445, f32[12,512,512]{1,2,0:T(8,128)} %fusion.206, f32[12,512,512]{1,2,0:T(8,128)} %fusion.207, f32[12,512]{1,0:T(8,128)S(1)} %dynamic-slice_bitcast_fusion.2, ...), kind=kOutput, calls=%fused_computation.28.clone.1 | convolution fusion | flops 2853181952 | bytes 67437568 | tf_op jit(solution)/shard_map/while/body/eval_jaxpr/hij,hje->hie/dot_general | solution.py:53
  427.6 7.2 bitcast_dynamic-update-slice_fusion.14
  434.9 12.2 %fusion.207 = f32[12,512,512]{1,2,0:T(8,128)} fusion(bf16[2,12,512,448]{2,3,1,0:T(8,128)(2,1)} %get-tuple-element.462, s32[]{:T(128)} %get-tuple-element.445, bf16[2,12,512,448]{2,3,1,0:T(8,128)(2,1)} %get-tuple-element.461), kind=kOutput, calls=%fused_computation.43.clone.1 | convolution fusion | flops 2818572288 | bytes 23593984 | tf_op jit(solution)/shard_map/while/body/eval_jaxpr/hie,hje->hij/dot_general | solution.py:29
  447.0 6.3 fusion.206
  453.6 27.7 %bitcast_dynamic-update-slice_fusion.13 = f32[2,12,512,448]{2,3,1,0:T(8,128)} fusion(f32[2,12,512,448]{2,3,1,0:T(8,128)} %get-tuple-element.447, s32[]{:T(128)} %get-tuple-element.445, bf16[2,12,512,448]{2,3,1,0:T(8,128)(2,1)} %get-tuple-element.461, f32[12,512,512]{1,2,0:T(8,128)} %fusion.206, f32[12,512,512]{1,2,0:T(8,128)} %fusion.207, ...), kind=kOutput, calls=%fused_computation.27.clone.1 | convolution fusion | flops 2853181952 | bytes 67437568 | tf_op jit(solution)/shard_map/while/body/eval_jaxpr/hij,hie->hje/dot_general | solution.py:56
  481.3 23.5 %bitcast_dynamic-update-slice_fusion.12 = f32[2,12,512,448]{2,3,1,0:T(8,128)} fusion(f32[2,12,512,448]{2,3,1,0:T(8,128)} %get-tuple-element.446, s32[]{:T(128)} %get-tuple-element.445, f32[12,512,512]{1,2,0:T(8,128)} %fusion.206, f32[12,512,512]{1,2,0:T(8,128)} %fusion.207, f32[12,512]{1,0:T(8,128)S(1)} %dynamic-slice_bitcast_fusion.2, ...), kind=kOutput, calls=%fused_computation.28.clone.1 | convolution fusion | flops 2853181952 | bytes 67437568 | tf_op jit(solution)/shard_map/while/body/eval_jaxpr/hij,hje->hie/dot_general | solution.py:53
  504.8 7.3 bitcast_dynamic-update-slice_fusion.14
  512.2 19.0 %slice_multiply_fusion.7 = (f32[2,12,512,192]{2,3,1,0:T(8,128)S(1)}, f32[2,12,512,192]{2,3,1,0:T(8,128)}, f32[2,12,512,192]{2,3,1,0:T(8,128)}, f32[2,12,512,192]{2,3,1,0:T(8,128)}) fusion(f32[2,12,512,448]{2,3,1,0:T(8,128)} %get-tuple-element.109, f32[2,512,192]{1,2,0:T(8,128)} %copy.173, f32[2,512,192]{1,2,0:T(8,128)} %copy.171, ...), kind=kLoop, calls=%fused_computation.114 | loop fusion | flops 9437184 | bytes 58195968 | tf_op jit(solution)/shard_map/mul | solution.py:252
  531.2 19.8 %fusion.111 = bf16[2,512,12,64]{1,3,2,0:T(8,128)(2,1)S(1)} fusion(f32[2,12,512,448]{2,3,1,0:T(8,128)} %get-tuple-element.110, f32[192,64]{0,1:T(8,128)S(1)} %copy-done.26, f32[192,64]{0,1:T(8,128)S(1)} %copy-done.27, f32[2,12,512,192]{2,3,1,0:T(8,128)} %get-tuple-element.271, f32[2,12,512,192]{2,3,1,0:T(8,128)} %get-tuple-element.272), kind=kOutput, calls=%fused_computation.152 | convolution fusion | flops 3630194688 | bytes 23691264 | tf_op jit(solution)/shard_map/rhlf,fd->rhld/dot_general | solution.py:257
  553.1 15.3 %fusion.110 = bf16[2,512,12,64]{1,3,2,0:T(8,128)(2,1)S(1)} fusion(f32[2,12,512,448]{2,3,1,0:T(8,128)} %get-tuple-element.109, f32[192,64]{0,1:T(8,128)S(1)} %copy-done.24, f32[192,64]{0,1:T(8,128)S(1)} %copy-done.25, f32[2,12,512,192]{2,3,1,0:T(8,128)} %get-tuple-element.264, f32[2,12,512,192]{2,3,1,0:T(8,128)S(1)} %get-tuple-element.263), kind=kOutput, calls=%fused_computation.151 | convolution fusion | flops 3630194688 | bytes 23691264 | tf_op jit(solution)/shard_map/rhlf,fd->rhld/dot_general | solution.py:254
  575.1 5.8 convolution_bitcast_fusion
  580.9 8.0 copy.223
  589.4 5.0 fusion.156
  594.5 10.7 fusion.143
  606.6 10.2 fusion.157
  617.0 98.3 %reduce-scatter.13.cloned.1.call-done = f32[96,2304]{1,0:T(8,128)} async-done(((f32[768,2304]{1,0:T(8,128)}), f32[96,2304]{1,0:T(8,128)}) %reduce-scatter.13.cloned.1.call-update) | async-done | bytes 884752 | tf_op jit(solution)/shard_map/reduce_scatter | solution.py:297
  720.2 13.1 %fusion.112 = f32[384,64]{0,1:T(8,128)S(1)} fusion(bf16[2,512,12,64]{1,0,3,2:T(2,128)(2,1)S(1)} %copy-done.10, f32[2,12,512,192]{2,3,1,0:T(8,128)} %get-tuple-element.271, f32[2,12,512,192]{2,3,1,0:T(8,128)} %get-tuple-element.272), kind=kOutput, calls=%fused_computation.153 | convolution fusion | flops 3628597248 | bytes 20545536 | tf_op jit(solution)/shard_map/rhld,rhlf->fd/dot_general | solution.py:266
  733.8 13.1 %fusion.117 = f32[384,64]{0,1:T(8,128)S(1)} fusion(bf16[2,512,12,64]{1,0,3,2:T(2,128)(2,1)S(1)} %copy-done.8, f32[2,12,512,192]{2,3,1,0:T(8,128)} %get-tuple-element.264, f32[2,12,512,192]{2,3,1,0:T(8,128)} %copy-done.1), kind=kOutput, calls=%fused_computation.154 | convolution fusion | flops 3628597248 | bytes 20545536 | tf_op jit(solution)/shard_map/rhld,rhlf->fd/dot_general | solution.py:260
  752.7 38.0 %all-reduce.24 = (bf16[2304]{0:T(1024)(128)(2,1)S(1)}, bf16[24576]{0:T(1024)(128)(2,1)S(1)}, bf16[768]{0:T(1024)(128)(2,1)S(1)}, bf16[768]{0:T(1024)(128)(2,1)S(...) all-reduce(f32[2304]{0:T(1024)S(1)} %convert_reduce_fusion.1, ...), channel_id=4, replica_groups=mesh['fsdp'=8,'rep'=4] {'fsdp'}, use_global_device_ids=true, to_apply=%region_18.19.clone | all-reduce | flops 34560 | bytes 207360
  791.3 10.3 all-reduce.18
  808.1 145.1 %reduce-scatter.9.cloned.1.call-done = f32[96,3072]{1,0:T(8,128)} async-done(((f32[768,3072]{1,0:T(8,128)}), f32[96,3072]{1,0:T(8,128)}) %reduce-scatter.9.cloned.1.call-update) | async-done | bytes 1179664 | tf_op jit(solution)/shard_map/reduce_scatter | solution.py:299
  955.3 162.7 %reduce-scatter.11.cloned.1.call-done = f32[384,768]{1,0:T(8,128)} async-done(((f32[3072,768]{1,0:T(8,128)}), f32[384,768]{1,0:T(8,128)}) %reduce-scatter.11.cloned.1.call-update) | async-done | bytes 1179664 | tf_op jit(solution)/shard_map/reduce_scatter | solution.py:300
  1120.2 8.6 add_convert_fusion.2
  1128.8 11.2 all-gather.16.cloned.1.call-done
  1142.7 40.4 %all-reduce.23.cloned.1.call-done = (bf16[96,768]{1,0:T(8,128)(2,1)}, bf16[96,3072]{1,0:T(8,128)(2,1)}, bf16[384,768]{1,0:T(8,128)(2,1)}) async-done(((bf16[96,768]{1,0:T(8,128)(2,1)}, bf16[96,3072]{1,0:T(8,128)(2,1)}, bf16[384,768]{1,0:T(8,128)(2,1)}), (bf16[96,768]{1,0:T(8,128)(2,1)}, bf16[96,3072]{1,0:T(8,128)(2,1)}, bf16[384,768]{1,0:T(8,128)(2,1)})) %all-reduce.23.cloned.1.call-update) | async-done | bytes 1327120 | tf_op jit(solution)/shard_map/psum | solution.py:315
  (295 shorter events, 123.0 us)
Async XLA Ops:
  7.2 125.1 %all-gather.8.cloned.1.call-start = ((), (), s32[]{:S(2)}) async-start(), calls=%async_computation.4 | async-start | bytes 3981312 | tf_op jit(solution)/shard_map/all_gather | solution.py:103
  7.9 249.5 %all-gather.10.cloned.1.call-start = ((), (), s32[]{:S(2)}) async-start(), calls=%async_computation.5 | async-start | bytes 1327104 | tf_op jit(solution)/shard_map/all_gather | solution.py:104
  8.7 253.1 %all-gather.12.cloned.1.call-start = ((), (), s32[]{:S(2)}) async-start(), calls=%async_computation.6 | async-start | bytes 5308416 | tf_op jit(solution)/shard_map/all_gather | solution.py:105
  9.4 288.6 %all-gather.14.cloned.1.call-start = ((), (), s32[]{:S(2)}) async-start(), calls=%async_computation.7 | async-start | bytes 5308416 | tf_op jit(solution)/shard_map/all_gather | solution.py:106
  10.0 705.2 %reduce-scatter.13.cloned.1.call-start = ((), (), s32[]{:S(2)}) async-start(), calls=%async_computation.12 | async-start | bytes 7962624 | tf_op jit(solution)/shard_map/reduce_scatter | solution.py:297
  94.6 5.5 copy-start.51
  96.0 36.3 %copy-start.52 = (bf16[2,512,768]{2,1,0:T(8,128)(2,1)S(1)}, bf16[2,512,768]{2,1,0:T(8,128)(2,1)}, u32[]{:S(2)}) copy-start(bf16[2,512,768]{2,1,0:T(8,128)(2,1)} %param.21) | copy-start | bytes 4718596
  100.1 243.1 %copy-start.33 = (f32[768]{0:T(1024)}, f32[768]{0:T(1024)S(1)}, u32[]{:S(2)}) copy-start(f32[768]{0:T(1024)S(1)} %convert_element_type.227) | copy-start | bytes 9220
  100.1 198.0 %copy-start.37 = (f32[768]{0:T(1024)}, f32[768]{0:T(1024)S(1)}, u32[]{:S(2)}) copy-start(f32[768]{0:T(1024)S(1)} %convert_element_type.228) | copy-start | bytes 9220
  154.8 6.7 copy-start.7
  154.9 6.7 copy-start.29
  154.9 6.7 copy-start.30
  188.3 12.5 %copy-start.35 = (s32[2,512]{1,0:T(2,128)S(1)}, s32[2,512]{1,0:T(2,128)}, u32[]{:S(2)}) copy-start(s32[2,512]{1,0:T(2,128)} %param.22) | copy-start | bytes 12292
  214.3 8.3 copy-start
  239.8 8.2 copy-start
  252.2 5.2 copy-start.4
  261.2 82.0 %copy-start.2 = (f32[1024,768]{1,0:T(8,128)}, f32[1024,768]{1,0:T(8,128)S(1)}, u32[]{:S(2)}) copy-start(f32[1024,768]{1,0:T(8,128)S(1)} %get-tuple-element.287) | copy-start | bytes 9437188
  261.3 81.9 %copy-start.20 = (f32[1024]{0:T(1024)}, f32[1024]{0:T(1024)S(1)}, u32[]{:S(2)}) copy-start(f32[1024]{0:T(1024)S(1)} %broadcast_multiply_fusion.1) | copy-start | bytes 12292
  261.8 81.4 %copy-start.22 = (f32[1024]{0:T(1024)}, f32[1024]{0:T(1024)S(1)}, u32[]{:S(2)}) copy-start(f32[1024]{0:T(1024)S(1)} %fusion.137) | copy-start | bytes 12292
  261.8 36.2 %copy-start.50 = (f32[768]{0:T(1024)S(1)}, f32[768]{0:T(1024)}, u32[]{:S(2)}) copy-start(f32[768]{0:T(1024)} %convert_element_type.232) | copy-start | bytes 9220
  298.1 9.7 copy-start.11
  298.1 9.7 copy-start.39
  349.8 7.3 copy-start.5
  349.8 7.3 copy-start.19
  349.8 7.3 copy-start.36
  512.2 19.0 %copy-start.26 = (f32[192,64]{0,1:T(8,128)S(1)}, f32[192,64]{0,1:T(8,128)}, u32[]{:S(2)}) copy-start(f32[192,64]{0,1:T(8,128)} %copy.191) | copy-start | bytes 147460
  512.2 19.0 %copy-start.27 = (f32[192,64]{0,1:T(8,128)S(1)}, f32[192,64]{0,1:T(8,128)}, u32[]{:S(2)}) copy-start(f32[192,64]{0,1:T(8,128)} %copy.190) | copy-start | bytes 147460
  531.2 21.9 %copy-start.1 = (f32[2,12,512,192]{2,3,1,0:T(8,128)}, f32[2,12,512,192]{2,3,1,0:T(8,128)S(1)}, u32[]{:S(2)}) copy-start(f32[2,12,512,192]{2,3,1,0:T(8,128)S(1)} %get-tuple-element.263) | copy-start | bytes 28311556
  588.9 5.5 copy-start.3
  589.0 5.5 copy-start.21
  589.0 5.5 copy-start.23
  589.0 5.5 copy-start.34
  589.0 5.5 copy-start.38
  589.0 217.4 %reduce-scatter.7.cloned.1.call-start = ((), (), s32[]{:S(2)}) async-start(), calls=%async_computation.8 | async-start | bytes 2654208 | tf_op jit(solution)/shard_map/reduce_scatter | solution.py:298
  594.4 358.7 %reduce-scatter.9.cloned.1.call-start = ((), (), s32[]{:S(2)}) async-start(), calls=%async_computation.9 | async-start | bytes 10616832 | tf_op jit(solution)/shard_map/reduce_scatter | solution.py:299
  605.2 512.8 %reduce-scatter.11.cloned.1.call-start = ((), (), s32[]{:S(2)}) async-start(), calls=%async_computation.10 | async-start | bytes 10616832 | tf_op jit(solution)/shard_map/reduce_scatter | solution.py:300
  616.9 100.4 %copy-start.12 = (bf16[2,512,768]{2,1,0:T(8,128)(2,1)S(1)}, bf16[2,512,768]{2,1,0:T(8,128)(2,1)}, u32[]{:S(2)}) copy-start(bf16[2,512,768]{2,1,0:T(8,128)(2,1)} %param.37) | copy-start | bytes 4718596
  616.9 103.3 %copy-start.10 = (bf16[2,512,12,64]{1,0,3,2:T(2,128)(2,1)S(1)}, bf16[2,512,12,64]{1,0,3,2:T(2,128)(2,1)}, u32[]{:S(2)}) copy-start(bf16[2,512,12,64]{1,0,3,2:T(2,128)(2,1)} %reshape.335) | copy-start | bytes 4718596
  616.9 523.1 %all-gather.16.cloned.1.call-start = ((), (), s32[]{:S(2)}) async-start(), calls=%async_computation.11 | async-start | bytes 2211840 | tf_op jit(solution)/shard_map/all_gather | solution.py:312
  717.2 466.0 %all-reduce.23.cloned.1.call-start = ((), (), s32[]{:S(2)}) async-start(), calls=%async_computation.13 | async-start | bytes 2654208 | tf_op jit(solution)/shard_map/psum | solution.py:315
  720.2 13.6 %copy-start.8 = (bf16[2,512,12,64]{1,0,3,2:T(2,128)(2,1)S(1)}, bf16[2,512,12,64]{1,0,3,2:T(2,128)(2,1)}, u32[]{:S(2)}) copy-start(bf16[2,512,12,64]{1,0,3,2:T(2,128)(2,1)} %reshape.333) | copy-start | bytes 4718596
  747.6 5.1 copy-start.41
  747.6 5.1 copy-start.45
  747.6 5.1 copy-start.46
  747.6 5.1 copy-start.48
  747.6 5.1 copy-start.49
  747.6 372.6 %copy-start.14 = (f32[1024,768]{1,0:T(8,128)S(1)}, f32[1024,768]{1,0:T(8,128)}, u32[]{:S(2)}) copy-start(f32[1024,768]{1,0:T(8,128)} %copy-done.13) | copy-start | bytes 9437188
  747.6 372.6 %copy-start.43 = (f32[1024]{0:T(1024)S(1)}, f32[1024]{0:T(1024)}, u32[]{:S(2)}) copy-start(f32[1024]{0:T(1024)} %copy-done.42) | copy-start | bytes 12292
  (18 other events, 46.2 us)
Sparse Core Ops, SparseCore 0:
  10.2 68.4 all-gather.7
  80.9 39.9 all-gather.9
  123.1 78.0 all-gather.11
  203.2 77.6 all-gather.13
  589.1 126.1 reduce-scatter.12
  718.6 69.2 reduce-scatter.6
  791.4 161.6 reduce-scatter.8
  956.8 161.2 reduce-scatter.10
  1120.1 19.8 all-gather.15
  1143.6 39.5 all-reduce.22
